TPU v7x, 256 devices: a whole 4x4x8 slice. The times are simulated.
256 devices in a mesh: row: 16 (over y_hi, x, core), col: 16 (over y_lo, z).
Axes of the slice: x: 4, y: 4 (y_hi: 2, y_lo: 2; y = y_hi * 2 + y_lo), z: 8, core: 2. Of those that a mesh axis runs over, the one named last changes fastest.
Arguments:
- pool: bfloat16 [32768, 128], P(('row', 'col')), may hold values from -6 to 6
- targets: bfloat16 [32768], P(('row', 'col')), may hold values from -15 to 15
- picks: int32 [4096], P(('row', 'col')), may hold values from 0 to 127
- inducing: float32 [8192, 128], replicated, may hold values from -6 to 6
- inv_sq_lengths: float32 [128], replicated, may hold values from 0.04 to 0.12
- prec_old: float32 [8192, 8192], P('row', 'col'), may hold values from -1 to 6, as said below
- mean_old: float32 [8192], P('row'), may hold values from -6 to 6
- panel: int32 [1], replicated, may hold values from 0 to 31
Outputs:
- prec_new: float32 [8192, 8192], P('row', 'col')
- mean_new: float32 [8192], P('row')
Inputs may be any that keep to these rules, and one draw needn't show every extreme that they name: `picks`: each entry indexes a row of the dataset block held by the same device as the entry. `prec_old`: symmetric and positive definite.
All inputs are finite; a program needn't handle non-finite values.
Results may differ from a plain program's by a relative error of at most 0.0028.
Values may be sent and summed in bfloat16 or wider, within the bound.
No kernel may reach another device: no remote copies, remote signals or barrier semaphores. Data moves between devices by JAX's collectives and lax.ppermute only.
A program may use at most 128 MiB of HBM per device.

v0:
```python
import jax
import jax.numpy as jnp
from jax import lax
from jax.sharding import Mesh
from jax.sharding import PartitionSpec as P

M = 8192
PB = 256
ROW_COL = ("row_0", "row_1", "row_2", "col_0", "col_1")
ROW = ("row_0", "row_1", "row_2")
COL = ("col_0", "col_1")
RATE = 0.5
EPSILON = 1e-05


def over_axes(value, axes):
    for axis in axes:
        value = lax.psum(value, axis)
    return value


def side_by_side(arrays, axis, dim, along):
    columns = [a.reshape(*a.shape[:along], -1) for a in arrays]
    both = jnp.concatenate(columns, axis=along)
    out, at, finished = (lax.all_gather(both, axis, axis=dim, tiled=True), 0, [])
    for a, column in zip(arrays, columns):
        slab = out[..., at : at + column.shape[along]]
        finished.append(slab.reshape(*slab.shape[:along], *a.shape[along:]))
        at += column.shape[along]
    return tuple(finished)


def in_blocks(value, dim, devices):
    shape = value.shape
    blocks = value.reshape(*shape[:dim], devices, shape[dim] // devices, *shape[dim + 1 :])
    return jnp.moveaxis(blocks, dim, 0)


def summed_on_arrival(value, axis, dim):
    blocks = in_blocks(value, dim, lax.axis_size(axis))
    arrived = lax.all_to_all(blocks, axis, split_axis=0, concat_axis=0, tiled=True)
    return arrived.sum(axis=0)


def picked(value, axis, root):
    return lax.dynamic_index_in_dim(lax.all_gather(value, axis), root, 0, keepdims=False)


def kernel_block(points, weights, sample_x):
    sample_f = sample_x.astype(jnp.float32)
    point_sq = jnp.sum(points * points * weights, axis=1)
    sample_sq = jnp.sum(sample_f * sample_f * weights, axis=1)
    cross_term = lax.dot_general(
        points * weights, sample_f, (((1,), (1,)), ((), ())), precision=lax.Precision.HIGHEST
    )
    return jnp.exp(-0.5 * (point_sq[:, None] + sample_sq[None, :] - 2.0 * cross_term)).astype(
        jnp.bfloat16
    )


def local_diag(gram_tile, row_base, col_base):
    row_ids = row_base + jnp.arange(gram_tile.shape[0], dtype=jnp.int32)
    col_ids = col_base + jnp.arange(gram_tile.shape[1], dtype=jnp.int32)
    on_diag = row_ids[:, None] == col_ids[None, :]
    return jnp.sum(jnp.where(on_diag, gram_tile, 0.0))


def diag_total(gram_tile, row_base, col_base):
    return over_axes(local_diag(gram_tile, row_base, col_base), ROW_COL)


def local(pool, targets, picks, inducing, inv_sq_lengths, prec_old, mean_old, panel):
    n_rows = lax.axis_size(ROW)
    n_cols = lax.axis_size(COL)
    my_row = lax.axis_index(ROW)
    my_col = lax.axis_index(COL)
    tile_rows, tile_cols = prec_old.shape
    batch_count = picks.shape[0] * n_rows * n_cols
    row_base = my_row * tile_rows
    col_base = my_col * tile_cols
    samples = jnp.take(pool, picks, axis=0)
    values = jnp.take(targets, picks, axis=0)
    group_x, group_y = side_by_side((samples, values), COL, 0, 1)
    features = kernel_block(inducing, inv_sq_lengths, group_x)
    feat_cols = lax.dynamic_slice_in_dim(features, col_base, tile_cols, 0)
    own_y = values.astype(jnp.float32)
    power_sum = over_axes(jnp.sum(own_y * own_y), ROW_COL)
    gram_tile = lax.psum_scatter(
        lax.dot_general(
            features, feat_cols, (((1,), (1,)), ((), ())), preferred_element_type=jnp.float32
        ),
        ROW,
        scatter_dimension=0,
        tiled=True,
    )
    fit_part = summed_on_arrival(
        jnp.dot(features, group_y, preferred_element_type=jnp.float32), ROW, 0
    )
    trace_sum = diag_total(gram_tile, row_base, col_base)
    trace_scale = trace_sum / M
    joined = (1.0 - RATE) * prec_old + RATE * gram_tile / trace_scale
    mean_mid = (1.0 - RATE) * mean_old + RATE * fit_part / jnp.sqrt(
        trace_scale * (power_sum / batch_count + EPSILON)
    )
    panel_start = panel[0] * PB
    owner_row = panel_start // tile_rows
    owner_col = panel_start // tile_cols
    offset_row = panel_start - owner_row * tile_rows
    offset_col = panel_start - owner_col * tile_cols
    zero_index = jnp.zeros((), jnp.int32)
    col_piece = lax.dynamic_slice(joined, (zero_index, offset_col), (tile_rows, PB))
    got_cols = picked(col_piece, COL, owner_col)
    row_piece = lax.dynamic_slice(joined, (offset_row, zero_index), (PB, tile_cols))
    mean_piece = lax.dynamic_slice(mean_mid, (offset_row,), (PB,))
    diag_piece = lax.dynamic_slice(got_cols, (offset_row, zero_index), (PB, PB))
    got_rows, got_mean, got_block = (
        picked(row_piece, ROW, owner_row),
        picked(mean_piece, ROW, owner_row),
        picked(diag_piece, ROW, owner_row),
    )
    factor = jnp.linalg.cholesky(got_block)
    identity = jnp.eye(PB, dtype=jnp.float32)
    inv_factor = lax.linalg.triangular_solve(factor, identity, left_side=True, lower=True)
    wide_rows = lax.dot_general(
        got_cols, inv_factor, (((1,), (1,)), ((), ())), precision=lax.Precision.HIGHEST
    )
    solved_rows = jnp.dot(inv_factor, got_rows, precision=lax.Precision.HIGHEST)
    head_part = jnp.dot(inv_factor, got_mean, precision=lax.Precision.HIGHEST)
    updated = joined - jnp.dot(wide_rows, solved_rows, precision=lax.Precision.HIGHEST)
    in_col = my_col == owner_col
    in_row = my_row == owner_row
    updated = jnp.where(
        in_col, lax.dynamic_update_slice(updated, wide_rows, (zero_index, offset_col)), updated
    )
    updated = jnp.where(
        in_row, lax.dynamic_update_slice(updated, solved_rows, (offset_row, zero_index)), updated
    )
    updated = jnp.where(
        jnp.logical_and(in_row, in_col),
        lax.dynamic_update_slice(updated, factor, (offset_row, offset_col)),
        updated,
    )
    mean_next = mean_mid - jnp.dot(wide_rows, head_part, precision=lax.Precision.HIGHEST)
    mean_next = jnp.where(
        in_row, lax.dynamic_update_slice(mean_next, head_part, (offset_row,)), mean_next
    )
    return (updated, mean_next)


def solution(mesh):
    split = Mesh(mesh.devices.reshape(2, 4, 2, 2, 8), ("row_0", "row_1", "row_2", "col_0", "col_1"))
    return jax.shard_map(
        local,
        mesh=split,
        in_specs=(P(ROW_COL, None), P(ROW_COL), P(ROW_COL), P(), P(), P(ROW, COL), P(ROW), P()),
        out_specs=(P(ROW, COL), P(ROW)),
        check_vma=False,
    )
```

profile of v0, /device:TPU:1, one launch (start us, length us, event | category | flops | bytes accessed | tf_op | source)
XLA Modules:
  0.0 518.6 jit_solution(1494398708425106980)
XLA Ops:
  11.3 30.8 %all_gather.25 = bf16[256,129]{1,0:T(8,128)(2,1)S(1)} all-gather(bf16[16,129]{1,0:T(8,128)(2,1)S(1)} %pad_maximum_fusion.4), channel_id=1, replica_groups=mesh['row_0'=2,'row_1'=4,'row_2'=2,'col_0'=2,'col_1'=8] {'col_0','col_1'}, dimensions={0}, use_global_device_ids=true | all-gather | bytes 70176 | tf_op jit(solution)/shard_map/all_gather | solution.py:25
  42.8 3.3 multiply_reduce_fusion
  46.2 5.9 %fusion.3 = bf16[8192,256]{1,0:T(8,128)(2,1)S(1)} fusion(f32[8192,128]{1,0:T(8,128)} %param.11, f32[256]{0:T(256)S(1)} %multiply_reduce_fusion.1, f32[8192]{0:T(1024)S(1)} %multiply_reduce_fusion, f32[128]{0:T(128)S(1)} %copy-done.5, bf16[256,129]{1,0:T(8,128)(2,1)S(1)} %all_gather.25), kind=kOutput, calls=%fused_computation.8 | convolution fusion | flops 3232759808 | bytes 8488448 | tf_op jit(solution)/shard_map/dot_general | solution.py:53
  52.1 1.9 copy-done.1
  54.0 8.1 %fusion.14 = f32[8192,512]{1,0:T(8,128)} fusion(bf16[8192,256]{1,0:T(8,128)(2,1)S(1)} %fusion.3, s32[]{:T(128)S(6)} %select_n.109), kind=kOutput, calls=%fused_computation.33 | convolution fusion | flops 2147483648 | bytes 21233668 | tf_op jit(solution)/shard_map/dot_general | solution.py:89
  62.9 156.7 %reduce-scatter.2.cloned.1.call-done = f32[512,512]{1,0:T(8,128)} async-done(((f32[8192,512]{1,0:T(8,128)}), f32[512,512]{1,0:T(8,128)}) %reduce-scatter.2.cloned.1.call-update) | async-done | bytes 1048592 | tf_op jit(solution)/shard_map/reduce_scatter | solution.py:88
  219.6 2.2 select_reduce_fusion
  221.8 5.9 %all-reduce.5 = (f32[]{:T(128)}, f32[]{:T(128)}) all-reduce(f32[]{:T(128)} %select_reduce_fusion, f32[]{:T(128)} %get-tuple-element.28), channel_id=1, replica_groups=mesh['row_0'=2,'row_1'=4,'row_2'=2,'col_0'=2,'col_1'=8] {'row_0'}, use_global_device_ids=true, to_apply=%region_4.5 | all-reduce | flops 2 | bytes 16 | tf_op jit(solution)/shard_map/psum | solution.py:18
  227.6 7.2 %all-reduce.2 = (f32[]{:T(128)}, f32[]{:T(128)}) all-reduce(f32[]{:T(128)} %get-tuple-element.26, f32[]{:T(128)} %get-tuple-element.27), channel_id=1, replica_groups=mesh['row_0'=2,'row_1'=4,'row_2'=2,'col_0'=2,'col_1'=8] {'row_1'}, use_global_device_ids=true, to_apply=%region_5.6 | all-reduce | flops 2 | bytes 16 | tf_op jit(solution)/shard_map/psum | solution.py:18
  234.8 7.7 %all-reduce.4 = (f32[]{:T(128)}, f32[]{:T(128)}) all-reduce(f32[]{:T(128)} %get-tuple-element.20, f32[]{:T(128)} %get-tuple-element.21), channel_id=1, replica_groups=mesh['row_0'=2,'row_1'=4,'row_2'=2,'col_0'=2,'col_1'=8] {'row_2'}, use_global_device_ids=true, to_apply=%region_6.7 | all-reduce | flops 2 | bytes 16 | tf_op jit(solution)/shard_map/psum | solution.py:18
  242.5 4.4 all-reduce.3
  246.9 14.3 %all-reduce.1 = (f32[]{:T(128)}, f32[]{:T(128)}) all-reduce(f32[]{:T(128)} %get-tuple-element.22, f32[]{:T(128)} %get-tuple-element.23), channel_id=1, replica_groups=mesh['row_0'=2,'row_1'=4,'row_2'=2,'col_0'=2,'col_1'=8] {'col_1'}, use_global_device_ids=true, to_apply=%region_8.9 | all-reduce | flops 2 | bytes 16 | tf_op jit(solution)/shard_map/psum | solution.py:18
  264.3 100.1 %all-gather.10.cloned.1.call-done = f32[8192,256]{1,0:T(8,128)} async-done(((f32[512,256]{1,0:T(8,128)}), f32[8192,256]{1,0:T(8,128)}) %all-gather.10.cloned.1.call-update) | async-done | bytes 8388624 | tf_op jit(solution)/shard_map/all_gather | solution.py:46
  367.2 3.4 fusion.37
  371.2 7.3 %all-to-all-start = ((f32[16,1,512]{2,1,0:T(1,128)}), f32[16,1,512]{2,1,0:T(1,128)S(1)}, u32[]{:S(2)}, u32[]{:S(2)}) async-start(f32[16,1,512]{2,1,0:T(1,128)} %all_to_all.6), calls=%async_computation.1 | async-start | bytes 65536 | tf_op jit(solution)/shard_map/all_to_all | solution.py:41
  378.5 7.2 %all-to-all-done = f32[16,1,512]{2,1,0:T(1,128)S(1)} async-done(((f32[16,1,512]{2,1,0:T(1,128)}), f32[16,1,512]{2,1,0:T(1,128)S(1)}, u32[]{:S(2)}, u32[]{:S(2)}) %all-to-all-start) | async-done | bytes 32800 | tf_op jit(solution)/shard_map/all_to_all | solution.py:41
  386.6 20.6 %all-gather.3 = f32[16,1,256]{2,1,0:T(1,128)S(1)} all-gather(f32[1,1,256]{2,1,0:T(1,128)S(1)} %bitcast.74), channel_id=4, replica_groups=mesh['row_0'=2,'row_1'=4,'row_2'=2,'col_0'=2,'col_1'=8] {'row_0','row_1'..., dimensions={0}, use_global_device_ids=true | all-gather | bytes 17408 | tf_op jit(solution)/shard_map/all_gather | solution.py:46
  407.2 19.5 %all-gather.8.cloned.1.call-done = f32[16,256,256]{2,1,0:T(8,128)} async-done(((f32[1,256,256]{2,1,0:T(8,128)}), f32[16,256,256]{2,1,0:T(8,128)}) %all-gather.8.cloned.1.call-update) | async-done | bytes 4194320 | tf_op jit(solution)/shard_map/all_gather | solution.py:46
  428.9 11.7 %cholesky.50 = f32[128,128]{1,0:T(8,128)S(1)} custom-call(f32[128,128]{1,0:T(8,128)S(1)} %cholesky.118), custom_call_target="Cholesky" | custom-call | tf_op jit(solution)/shard_map/jit(cholesky)/cholesky | solution.py:121
  440.6 9.8 %custom-call.14 = f32[1,128,128]{1,2,0:T(8,128)S(1)} custom-call(f32[1,128,128]{2,1,0:T(8,128)S(1)} %get-tuple-element.35), custom_call_target="InvertDiagBlocksLowerTriangular" | custom-call | tf_op jit(solution)/shard_map/jit(cholesky)/cholesky | solution.py:121
  450.9 11.7 %cholesky.105 = f32[128,128]{1,0:T(8,128)S(1)} custom-call(f32[128,128]{1,0:T(8,128)S(1)} %convolution_subtract_fusion.2), custom_call_target="Cholesky" | custom-call | tf_op jit(solution)/shard_map/jit(cholesky)/cholesky | solution.py:121
  465.3 4.0 while.1
  469.3 19.7 %custom-call.15 = f32[2,128,128]{1,2,0:T(8,128)S(1)} custom-call(f32[2,128,128]{2,1,0:T(8,128)S(1)} %get-tuple-element.9), custom_call_target="InvertDiagBlocksLowerTriangular" | custom-call | tf_op jit(solution)/shard_map/triangular_solve | solution.py:123
  492.4 15.1 %all-gather.12.cloned.1.call-done = f32[4096,512]{1,0:T(8,128)} async-done(((f32[256,512]{1,0:T(8,128)}), f32[4096,512]{1,0:T(8,128)}) %all-gather.12.cloned.1.call-update) | async-done | bytes 8388624 | tf_op jit(solution)/shard_map/all_gather | solution.py:46
  (78 shorter events, 26.6 us)
Async XLA Ops:
  7.2 3.4 copy-start
  7.2 39.0 %copy-start.5 = (f32[128]{0:T(128)S(1)}, f32[128]{0:T(128)}, u32[]{:S(2)}) copy-start(f32[128]{0:T(128)} %param.12) | copy-start | bytes 1540
  7.2 212.4 %reduce-scatter.2.cloned.1.call-start = ((), (), s32[]{:S(2)}) async-start(), calls=%async_computation.2 | async-start | bytes 17825792 | tf_op jit(solution)/shard_map/reduce_scatter | solution.py:88
  52.1 1.9 copy-start.1
  62.1 199.8 %copy-start.3 = (f32[512,512]{1,0:T(8,128)S(1)}, f32[512,512]{1,0:T(8,128)}, u32[]{:S(2)}) copy-start(f32[512,512]{1,0:T(8,128)} %param.13) | copy-start | bytes 3145732
  62.1 302.3 %all-gather.10.cloned.1.call-start = ((), (), s32[]{:S(2)}) async-start(), calls=%async_computation.4 | async-start | bytes 8912896 | tf_op jit(solution)/shard_map/all_gather | solution.py:46
  263.4 123.1 %copy-start.6 = (f32[512]{0:T(512)S(1)}, f32[512]{0:T(512)}, u32[]{:S(2)}) copy-start(f32[512]{0:T(512)} %param.14) | copy-start | bytes 6148
  264.3 162.5 %all-gather.8.cloned.1.call-start = ((), (), s32[]{:S(2)}) async-start(), calls=%async_computation.3 | async-start | bytes 4456448 | tf_op jit(solution)/shard_map/all_gather | solution.py:46
  366.1 141.3 %all-gather.12.cloned.1.call-start = ((), (), s32[]{:S(2)}) async-start(), calls=%async_computation.5 | async-start | bytes 8912896 | tf_op jit(solution)/shard_map/all_gather | solution.py:46
  371.2 14.6 %all-to-all-start = ((f32[16,1,512]{2,1,0:T(1,128)}), f32[16,1,512]{2,1,0:T(1,128)S(1)}, u32[]{:S(2)}, u32[]{:S(2)}) async-start(f32[16,1,512]{2,1,0:T(1,128)} %all_to_all.6), calls=%async_computation.1 | async-start | bytes 65536 | tf_op jit(solution)/shard_map/all_to_all | solution.py:41
  510.5 0.6 copy-start.4
  511.1 1.0 copy-start.2
Sparse Core Ops, SparseCore 0:
  62.2 157.3 reduce-scatter.1
  264.4 100.0 all-gather.9
  367.2 59.5 all-gather.7
  429.9 77.4 all-gather.11
where the time goes:
time: 519 us
  waiting for transfers between devices  299 us (58%)
  blocking collectives  90.9 us (18%)
  other arithmetic  65.6 us (13%)
  matrix products  23.8 us (5%)
  between operations  17.4 us (3%)
  local copies, waits for them, and re-layouts  14.6 us (3%)
  starting transfers between devices  7.43 us (1%)
    reduce_scatter x1, waiting for transfers between devices, local(): lax.psum_scatter(lax.dot_general(features, feat_cols, (((1,), (1,)), ((),...  157 us
    all_gather x3, waiting for transfers between devices, picked(): lax.all_gather(value, axis)  135 us
    psum x5, blocking collectives, over_axes(): value = lax.psum(value, axis)  39.5 us
    another operation x7, other arithmetic, local(): factor = jnp.linalg.cholesky(got_block)  34.6 us
    all_gather x1, blocking collectives, side_by_side(): lax.all_gather(both, axis, axis=dim, tiled=True)  30.8 us
    all_gather x1, blocking collectives, picked(): lax.all_gather(value, axis)  20.6 us
    another operation x3, other arithmetic, local(): lax.linalg.triangular_solve(factor, identity, left_side=True, lower=True)  19.7 us
  transfers between devices with their start and end apart: 5, of which 5 were waited for; matrix products, arithmetic and copies ran while one was open for 13% of the time, Pallas kernels for 0%

commit v1 on v0

--- a/solution.py
+++ b/solution.py
@@ -15,7 +15,8 @@
 
 def over_axes(value, axes):
     for axis in axes:
-        value = lax.psum(value, axis)
+        shards = lax.all_gather(value, axis)
+        value = jnp.sum(shards, axis=0)
     return value
 
 

time: 519 us -> 537 us (1.035)
  local copies, waits for them, and re-layouts: 14.6 us -> 31.5 us
  other arithmetic: 65.6 us -> 71.9 us
    psum x5 -> x0, blocking collectives: 39.5 us -> none  [over_axes(): value = lax.psum(value, axis)]
    unnamed x0 -> x5, blocking collectives: none -> 36.3 us
    unnamed x14 -> x49, local copies, waits for them, and re-layouts: 3.43 us -> 20.4 us
    reduce_sum x0 -> x10, other arithmetic: none -> 6.29 us  [over_axes(): value = jnp.sum(shards, axis=0)]
where the time goes in v1:
time: 537 us; the launch traced here: 536 us
  waiting for transfers between devices  296 us (55%)
  blocking collectives  87.7 us (16%)
  other arithmetic  71.9 us (13%)
  local copies, waits for them, and re-layouts  31.5 us (6%)
  matrix products  23.8 us (4%)
  between operations  17.5 us (3%)
  starting transfers between devices  7.43 us (1%)
    reduce_scatter x1, waiting for transfers between devices, local(): lax.psum_scatter(lax.dot_general(features, feat_cols, (((1,), (1,)), ((),...  155 us
    all_gather x3, waiting for transfers between devices, picked(): lax.all_gather(value, axis)  134 us
    unnamed x5, blocking collectives  36.3 us
    another operation x7, other arithmetic, local(): factor = jnp.linalg.cholesky(got_block)  34.6 us
    all_gather x1, blocking collectives, side_by_side(): lax.all_gather(both, axis, axis=dim, tiled=True)  30.8 us
    all_gather x1, blocking collectives, picked(): lax.all_gather(value, axis)  20.6 us
    unnamed x49, local copies, waits for them, and re-layouts  20.4 us
    another operation x3, other arithmetic, local(): lax.linalg.triangular_solve(factor, identity, left_side=True, lower=True)  19.7 us
  transfers between devices with their start and end apart: 5, of which 5 were waited for; matrix products, arithmetic and copies ran while one was open for 13% of the time, Pallas kernels for 0%

profile of v1, /device:TPU:1, one launch (start us, length us, event | category | flops | bytes accessed | tf_op | source)
XLA Modules:
  0.0 536.1 jit_solution(396388877098088223)
XLA Ops:
  11.3 30.8 %all_gather.85 = bf16[256,129]{1,0:T(8,128)(2,1)S(1)} all-gather(bf16[16,129]{1,0:T(8,128)(2,1)S(1)} %pad_maximum_fusion.4), channel_id=1, replica_groups=mesh['row_0'=2,'row_1'=4,'row_2'=2,'col_0'=2,'col_1'=8] {'col_0','col_1'}, dimensions={0}, use_global_device_ids=true | all-gather | bytes 70176 | tf_op jit(solution)/shard_map/all_gather | solution.py:26
  42.8 3.3 multiply_reduce_fusion
  46.2 5.9 %fusion.3 = bf16[8192,256]{1,0:T(8,128)(2,1)S(1)} fusion(f32[8192,128]{1,0:T(8,128)} %param.11, f32[256]{0:T(256)S(1)} %multiply_reduce_fusion.1, f32[8192]{0:T(1024)S(1)} %multiply_reduce_fusion, f32[128]{0:T(128)S(1)} %copy-done.5, bf16[256,129]{1,0:T(8,128)(2,1)S(1)} %all_gather.85), kind=kOutput, calls=%fused_computation.8 | convolution fusion | flops 3232759808 | bytes 8488448 | tf_op jit(solution)/shard_map/dot_general | solution.py:54
  52.1 1.9 copy-done.1
  54.0 8.1 %fusion.14 = f32[8192,512]{1,0:T(8,128)} fusion(bf16[8192,256]{1,0:T(8,128)(2,1)S(1)} %fusion.3, s32[]{:T(128)S(6)} %select_n.109), kind=kOutput, calls=%fused_computation.33 | convolution fusion | flops 2147483648 | bytes 21233668 | tf_op jit(solution)/shard_map/dot_general | solution.py:90
  65.0 154.7 %reduce-scatter.2.cloned.1.call-done = f32[512,512]{1,0:T(8,128)} async-done(((f32[8192,512]{1,0:T(8,128)}), f32[512,512]{1,0:T(8,128)}) %reduce-scatter.2.cloned.1.call-update) | async-done | bytes 1048592 | tf_op jit(solution)/shard_map/reduce_scatter | solution.py:89
  219.6 2.2 select_reduce_fusion
  223.8 5.3 all-reduce.15
  233.7 6.5 %all-reduce.12 = (f32[4]{0:T(128)S(1)}, f32[4]{0:T(128)S(1)}) all-reduce(f32[4]{0:T(128)S(1)} %dynamic-update-slice.16, f32[4]{0:T(128)S(1)} %dynamic-update-slice.21), channel_id=1, replica_groups=mesh['row_0'=2,'row_1'=4,'row_2'=2,'col_0'=2,'col_1'=8] {'row_1'}, use_global_device_ids=true, to_apply=%add.2 | all-reduce | flops 8 | bytes 64
  244.9 7.1 %all-reduce.14 = (f32[2]{0:T(128)S(1)}, f32[2]{0:T(128)S(1)}) all-reduce(f32[2]{0:T(128)S(1)} %dynamic-update-slice.17, f32[2]{0:T(128)S(1)} %dynamic-update-slice.22), channel_id=1, replica_groups=mesh['row_0'=2,'row_1'=4,'row_2'=2,'col_0'=2,'col_1'=8] {'row_2'}, use_global_device_ids=true, to_apply=%add.3 | all-reduce | flops 4 | bytes 32
  256.6 3.8 all-reduce.13
  264.5 13.7 %all-reduce.11 = (f32[8]{0:T(128)S(1)}, f32[8]{0:T(128)S(1)}) all-reduce(f32[8]{0:T(128)S(1)} %dynamic-update-slice.19, f32[8]{0:T(128)S(1)} %dynamic-update-slice.24), channel_id=1, replica_groups=mesh['row_0'=2,'row_1'=4,'row_2'=2,'col_0'=2,'col_1'=8] {'col_1'}, use_global_device_ids=true, to_apply=%add.5 | all-reduce | flops 16 | bytes 128
  281.8 100.1 %all-gather.10.cloned.1.call-done = f32[8192,256]{1,0:T(8,128)} async-done(((f32[512,256]{1,0:T(8,128)}), f32[8192,256]{1,0:T(8,128)}) %all-gather.10.cloned.1.call-update) | async-done | bytes 8388624 | tf_op jit(solution)/shard_map/all_gather | solution.py:47
  384.7 3.4 fusion.37
  388.7 7.3 %all-to-all-start = ((f32[16,1,512]{2,1,0:T(1,128)}), f32[16,1,512]{2,1,0:T(1,128)S(1)}, u32[]{:S(2)}, u32[]{:S(2)}) async-start(f32[16,1,512]{2,1,0:T(1,128)} %all_to_all.6), calls=%async_computation.1 | async-start | bytes 65536 | tf_op jit(solution)/shard_map/all_to_all | solution.py:42
  396.0 7.2 %all-to-all-done = f32[16,1,512]{2,1,0:T(1,128)S(1)} async-done(((f32[16,1,512]{2,1,0:T(1,128)}), f32[16,1,512]{2,1,0:T(1,128)S(1)}, u32[]{:S(2)}, u32[]{:S(2)}) %all-to-all-start) | async-done | bytes 32800 | tf_op jit(solution)/shard_map/all_to_all | solution.py:42
  404.7 20.6 %all-gather.3 = f32[16,1,256]{2,1,0:T(1,128)S(1)} all-gather(f32[1,1,256]{2,1,0:T(1,128)S(1)} %bitcast.89), channel_id=4, replica_groups=mesh['row_0'=2,'row_1'=4,'row_2'=2,'col_0'=2,'col_1'=8] {'row_0','row_1'..., dimensions={0}, use_global_device_ids=true | all-gather | bytes 17408 | tf_op jit(solution)/shard_map/all_gather | solution.py:47
  425.3 18.9 %all-gather.8.cloned.1.call-done = f32[16,256,256]{2,1,0:T(8,128)} async-done(((f32[1,256,256]{2,1,0:T(8,128)}), f32[16,256,256]{2,1,0:T(8,128)}) %all-gather.8.cloned.1.call-update) | async-done | bytes 4194320 | tf_op jit(solution)/shard_map/all_gather | solution.py:47
  446.4 11.7 %cholesky.50 = f32[128,128]{1,0:T(8,128)S(1)} custom-call(f32[128,128]{1,0:T(8,128)S(1)} %cholesky.118), custom_call_target="Cholesky" | custom-call | tf_op jit(solution)/shard_map/jit(cholesky)/cholesky | solution.py:122
  458.1 9.8 %custom-call.14 = f32[1,128,128]{1,2,0:T(8,128)S(1)} custom-call(f32[1,128,128]{2,1,0:T(8,128)S(1)} %get-tuple-element.35), custom_call_target="InvertDiagBlocksLowerTriangular" | custom-call | tf_op jit(solution)/shard_map/jit(cholesky)/cholesky | solution.py:122
  468.4 11.7 %cholesky.105 = f32[128,128]{1,0:T(8,128)S(1)} custom-call(f32[128,128]{1,0:T(8,128)S(1)} %convolution_subtract_fusion.2), custom_call_target="Cholesky" | custom-call | tf_op jit(solution)/shard_map/jit(cholesky)/cholesky | solution.py:122
  482.8 4.0 while.1
  486.8 19.7 %custom-call.15 = f32[2,128,128]{1,2,0:T(8,128)S(1)} custom-call(f32[2,128,128]{2,1,0:T(8,128)S(1)} %get-tuple-element.9), custom_call_target="InvertDiagBlocksLowerTriangular" | custom-call | tf_op jit(solution)/shard_map/triangular_solve | solution.py:124
  509.9 15.1 %all-gather.12.cloned.1.call-done = f32[4096,512]{1,0:T(8,128)} async-done(((f32[256,512]{1,0:T(8,128)}), f32[4096,512]{1,0:T(8,128)}) %all-gather.12.cloned.1.call-update) | async-done | bytes 8388624 | tf_op jit(solution)/shard_map/all_gather | solution.py:47
  (123 shorter events, 49.8 us)
Async XLA Ops:
  7.2 3.4 copy-start
  7.2 39.0 %copy-start.5 = (f32[128]{0:T(128)S(1)}, f32[128]{0:T(128)}, u32[]{:S(2)}) copy-start(f32[128]{0:T(128)} %param.12) | copy-start | bytes 1540
  7.2 212.5 %reduce-scatter.2.cloned.1.call-start = ((), (), s32[]{:S(2)}) async-start(), calls=%async_computation.2 | async-start | bytes 17825792 | tf_op jit(solution)/shard_map/reduce_scatter | solution.py:89
  52.1 1.9 copy-start.1
  62.1 0.9 copy-start.11
  62.1 161.1 %copy-start.10 = (u32[256]{0:T(256)S(1)}, u32[256]{0:T(256)}, u32[]{:S(2)}) copy-start(u32[256]{0:T(256)} %constant.228) | copy-start | bytes 3076
  62.1 171.0 %copy-start.9 = (u32[256]{0:T(256)S(1)}, u32[256]{0:T(256)}, u32[]{:S(2)}) copy-start(u32[256]{0:T(256)} %constant.233) | copy-start | bytes 3076
  62.1 182.2 %copy-start.8 = (u32[256]{0:T(256)S(1)}, u32[256]{0:T(256)}, u32[]{:S(2)}) copy-start(u32[256]{0:T(256)} %constant.238) | copy-start | bytes 3076
  62.1 194.0 %copy-start.7 = (u32[256]{0:T(256)S(1)}, u32[256]{0:T(256)}, u32[]{:S(2)}) copy-start(u32[256]{0:T(256)} %constant.243) | copy-start | bytes 3076
  62.1 217.3 %copy-start.3 = (f32[512,512]{1,0:T(8,128)S(1)}, f32[512,512]{1,0:T(8,128)}, u32[]{:S(2)}) copy-start(f32[512,512]{1,0:T(8,128)} %param.13) | copy-start | bytes 3145732
  62.1 319.8 %all-gather.10.cloned.1.call-start = ((), (), s32[]{:S(2)}) async-start(), calls=%async_computation.4 | async-start | bytes 8912896 | tf_op jit(solution)/shard_map/all_gather | solution.py:47
  280.9 123.7 %copy-start.6 = (f32[512]{0:T(512)S(1)}, f32[512]{0:T(512)}, u32[]{:S(2)}) copy-start(f32[512]{0:T(512)} %param.14) | copy-start | bytes 6148
  281.8 162.5 %all-gather.8.cloned.1.call-start = ((), (), s32[]{:S(2)}) async-start(), calls=%async_computation.3 | async-start | bytes 4456448 | tf_op jit(solution)/shard_map/all_gather | solution.py:47
  383.6 141.3 %all-gather.12.cloned.1.call-start = ((), (), s32[]{:S(2)}) async-start(), calls=%async_computation.5 | async-start | bytes 8912896 | tf_op jit(solution)/shard_map/all_gather | solution.py:47
  388.7 14.6 %all-to-all-start = ((f32[16,1,512]{2,1,0:T(1,128)}), f32[16,1,512]{2,1,0:T(1,128)S(1)}, u32[]{:S(2)}, u32[]{:S(2)}) async-start(f32[16,1,512]{2,1,0:T(1,128)} %all_to_all.6), calls=%async_computation.1 | async-start | bytes 65536 | tf_op jit(solution)/shard_map/all_to_all | solution.py:42
  528.0 0.6 copy-start.4
  528.6 1.0 copy-start.2
Sparse Core Ops, SparseCore 0:
  62.3 157.3 reduce-scatter.1
  281.9 100.0 all-gather.9
  384.7 59.5 all-gather.7
  447.4 77.4 all-gather.11
